TPU v7x, 128 devices: a whole 4x4x4 slice. The times are simulated.
128 devices in a mesh: req: 32 (over y, x, core), mlp: 4 (over z).
Axes of the slice: x: 4, y: 4, z: 4, core: 2. Of those that a mesh axis runs over, the one named last changes fastest.
Arguments:
- tokens: bfloat16 [8192, 2560], P('req'), may hold values from -125 to 125
- lengths: int32 [32, 4], P('req'), may hold values from 1 to 128, 256 in all within a row
- page_table: int32 [32, 16], P('req'), may hold values from 0 to 15, each once within a row
- attn_norm: float32 [2560], replicated, may hold values from 0.25 to 1.75
- qkv_weight: bfloat16 [2560, 8, 768], P(None, 'mlp'), may hold values from -0.125 to 0.125
- q_norm: float32 [128], replicated, may hold values from 0.25 to 1.75
- k_norm: float32 [128], replicated, may hold values from 0.25 to 1.75
- o_weight: bfloat16 [4096, 2560], P('mlp'), may hold values from -0.09375 to 0.09375
- mlp_norm: float32 [2560], replicated, may hold values from 0.25 to 1.75
- gate_up: bfloat16 [9728, 2, 2560], P(('req', 'mlp')), may hold values from -0.125 to 0.125
- down_weight: bfloat16 [9728, 2560], P(('req', 'mlp')), may hold values from -0.0625 to 0.0625
Outputs:
- layer_out: bfloat16 [8192, 2560], P(('req', 'mlp'))
- kv_cache: bfloat16 [2, 512, 16, 8, 128], P(None, 'req', None, 'mlp')
Inputs may be any that keep to these rules, and one draw needn't show every extreme that they name: `lengths`: each row sums to 256, and the longest prompt of every pack is exactly 128. `page_table`: each row is a permutation of 0 .. 15.
All inputs are finite; a program needn't handle non-finite values.
Results may differ from a plain program's by a relative error of at most 0.0049.
Values may be sent and summed in bfloat16 or wider, within the bound.
No kernel may reach another device: no remote copies, remote signals or barrier semaphores. Data moves between devices by JAX's collectives and lax.ppermute only.
A program may use at most 128 MiB of HBM per device.

v0:
```python
import math
import jax
import jax.numpy as jnp
from jax import lax
from jax.sharding import PartitionSpec as P

rope_theta = 1000000.0
norm_eps = 1e-06


def rms_scale(values, gain):
    mean_sq = jnp.mean(values * values, axis=-1, keepdims=True)
    return values * lax.rsqrt(mean_sq + norm_eps) * gain


def positions_of(lengths, slots):
    ends = jnp.cumsum(lengths)
    slot_ids = jnp.arange(slots, dtype=jnp.int32)
    passed = (ends[None, :] <= slot_ids[:, None]).astype(jnp.int32)
    segment = jnp.sum(passed, axis=1)
    start = jnp.sum(passed * lengths[None, :], axis=1)
    return (slot_ids, segment, slot_ids - start)


def rotate(values, position, head_dim):
    half = head_dim // 2
    freq = rope_theta ** (-(2.0 * jnp.arange(half, dtype=jnp.float32)) / head_dim)
    angle = position.astype(jnp.float32)[:, None] * freq[None, :]
    shape = (angle.shape[0],) + (1,) * (values.ndim - 2) + (half,)
    cosine = jnp.cos(angle).reshape(shape)
    sine = jnp.sin(angle).reshape(shape)
    first = values[..., :half]
    second = values[..., half:]
    return jnp.concatenate(
        [first * cosine - second * sine, second * cosine + first * sine], axis=-1
    )


def feed_forward(rows, unit_pairs, unit_down):
    gate = jnp.einsum("td,fd->tf", rows, unit_pairs[:, 0, :], preferred_element_type=jnp.float32)
    upper = jnp.einsum("td,fd->tf", rows, unit_pairs[:, 1, :], preferred_element_type=jnp.float32)
    act = (jax.nn.silu(gate) * upper).astype(jnp.bfloat16)
    return jnp.dot(act, unit_down, preferred_element_type=jnp.float32)


def per_device(
    tokens,
    lengths,
    page_table,
    attn_norm,
    qkv_weight,
    q_norm,
    k_norm,
    o_weight,
    mlp_norm,
    gate_up,
    down_weight,
):
    slots = tokens.shape[0]
    head_dim = q_norm.shape[0]
    local_kv = qkv_weight.shape[1]
    group_q = qkv_weight.shape[2] // head_dim - 2
    pages = page_table.shape[1]
    page_rows = slots // pages
    owned = slots // lax.axis_size("mlp")
    slot_ids, segment, position = positions_of(lengths[0], slots)
    normed = rms_scale(tokens.astype(jnp.float32), attn_norm).astype(jnp.bfloat16)
    qkv = jnp.einsum("sd,dkc->skc", normed, qkv_weight, preferred_element_type=jnp.float32)
    query = qkv[:, :, : group_q * head_dim].reshape(slots, local_kv, group_q, head_dim)
    key = qkv[:, :, group_q * head_dim : (group_q + 1) * head_dim]
    value = qkv[:, :, (group_q + 1) * head_dim :]
    query = rotate(rms_scale(query, q_norm), position, head_dim).astype(jnp.bfloat16)
    key = rotate(rms_scale(key, k_norm), position, head_dim).astype(jnp.bfloat16)
    value = value.astype(jnp.bfloat16)
    key_pages = key.reshape(pages, page_rows, local_kv, head_dim)
    value_pages = value.reshape(pages, page_rows, local_kv, head_dim)
    kv_cache = jnp.zeros((2, pages, page_rows, local_kv, head_dim), jnp.bfloat16)
    kv_cache = kv_cache.at[:, page_table[0]].set(jnp.stack([key_pages, value_pages]))
    scores = jnp.einsum(
        "skgd,tkd->kgst", query, key, preferred_element_type=jnp.float32
    ) / math.sqrt(head_dim)
    allowed = (segment[:, None] == segment[None, :]) & (slot_ids[None, :] <= slot_ids[:, None])
    weights = jnp.where(allowed, jnp.exp(scores), 0.0)
    probs = (weights / jnp.sum(weights, axis=-1, keepdims=True)).astype(jnp.bfloat16)
    context = jnp.einsum("kgst,tkd->skgd", probs, value, preferred_element_type=jnp.float32)
    context = context.astype(jnp.bfloat16).reshape(slots, local_kv * group_q * head_dim)
    piece = context
    attn_out = lax.psum_scatter(
        jnp.dot(piece, o_weight, preferred_element_type=jnp.float32),
        "mlp",
        scatter_dimension=0,
        tiled=True,
    )
    mine = lax.dynamic_slice_in_dim(tokens, lax.axis_index("mlp") * owned, owned, 0).astype(
        jnp.float32
    )
    resid = mine + attn_out
    mlp_in = rms_scale(resid, mlp_norm).astype(jnp.bfloat16)
    unit_pairs, unit_down = (
        lax.all_gather(gate_up, "mlp", axis=0, tiled=True),
        lax.all_gather(down_weight, "mlp", axis=0, tiled=True),
    )
    gathered = lax.all_gather(mlp_in, "req", axis=0, tiled=True)
    piece = gathered
    mlp_out = lax.psum_scatter(
        feed_forward(piece, unit_pairs, unit_down).astype(jnp.bfloat16),
        "req",
        scatter_dimension=0,
        tiled=True,
    ).astype(jnp.float32)
    layer_out = (resid + mlp_out).astype(jnp.bfloat16)
    return (layer_out, kv_cache)


def solution(mesh):
    return jax.shard_map(
        per_device,
        mesh=mesh,
        in_specs=(
            P("req", None),
            P("req", None),
            P("req", None),
            P(),
            P(None, "mlp", None),
            P(),
            P(),
            P("mlp", None),
            P(),
            P(("req", "mlp"), None, None),
            P(("req", "mlp"), None),
        ),
        out_specs=(P(("req", "mlp"), None), P(None, "req", None, "mlp", None)),
        check_vma=False,
    )
```

profile of v0, /device:TPU:0, one launch (start us, length us, event | category | flops | bytes accessed | tf_op | source)
XLA Modules:
  0.0 324.5 jit_solution(15002400929183191970)
XLA Ops:
  7.2 1.7 fusion.3
  8.9 5.9 %fusion = f32[256,2,768]{2,0,1:T(8,128)S(1)} fusion(bf16[2560,2,768]{2,1,0:T(2,128)(2,1)} %param.15, bf16[256,2560]{1,0:T(8,128)(2,1)} %param.11, f32[2560]{0:T(1024)} %param.14, f32[256]{0:T(256)S(1)} %add_rsqrt_fusion.2), kind=kOutput, calls=%fused_computation.2 | convolution fusion | flops 2015887360 | bytes 10759168 | tf_op jit(solution)/shard_map/sd,dkc->skc/dot_general | solution.py:68
  15.0 1.0 copy-done.2
  18.3 1.1 multiply_multiply_fusion
  20.4 0.8 fusion.6
  21.3 1.7 convolution_convert_fusion.1
  23.8 3.1 fusion.30
  26.9 0.7 all-gather.9.cloned.1.call-update
  27.7 0.7 all-gather.7.cloned.1.call-update
  28.4 35.3 %reduce-scatter.3.cloned.1.call-done = f32[64,2560]{1,0:T(8,128)} async-done(((f32[256,2560]{1,0:T(8,128)}), f32[64,2560]{1,0:T(8,128)}) %reduce-scatter.3.cloned.1.call-update) | async-done | bytes 655376 | tf_op jit(solution)/shard_map/reduce_scatter | solution.py:88
  63.8 1.3 multiply_reduce_fusion.1
  65.1 1.9 multiply_convert_fusion
  67.3 25.0 %all-gather.9.cloned.1.call-done = bf16[4,76,2560]{2,1,0:T(8,128)(2,1)} async-done(((bf16[1,76,2560]{2,1,0:T(8,128)(2,1)}), bf16[4,76,2560]{2,1,0:T(8,128)(2,1)}) %all-gather.9.cloned.1.call-update) | async-done | bytes 1556496 | tf_op jit(solution)/shard_map/all_gather | solution.py:101
  92.2 1.6 reshape.257
  93.8 39.3 %all-gather.7.cloned.1.call-done = bf16[304,2,2560]{2,1,0:T(2,128)(2,1)} async-done(((bf16[76,2,2560]{2,1,0:T(2,128)(2,1)}), bf16[304,2,2560]{2,1,0:T(2,128)(2,1)}) %all-gather.7.cloned.1.call-update) | async-done | bytes 3112976 | tf_op jit(solution)/shard_map/all_gather | solution.py:100
  133.1 9.4 %fusion.27 = (bf16[304,1,2560]{2,1,0:T(2,128)(2,1)}, bf16[304,1,2560]{2,1,0:T(2,128)(2,1)}) fusion(bf16[304,2,2560]{2,1,0:T(2,128)(2,1)} %all-gather.7.cloned.1.call-done), kind=kLoop, calls=%fused_computation.66 | loop fusion | bytes 6225920 | tf_op jit(solution)/shard_map/slice | solution.py:41
  142.6 50.8 %all-gather.5.cloned.1.call-done = bf16[2048,2560]{1,0:T(8,128)(2,1)} async-done(((bf16[64,2560]{1,0:T(8,128)(2,1)}), bf16[2048,2560]{1,0:T(8,128)(2,1)}) %all-gather.5.cloned.1.call-update) | async-done | bytes 10485776 | tf_op jit(solution)/shard_map/all_gather | solution.py:103
  193.4 9.8 %fusion.7 = f32[2048,304]{0,1:T(8,128)} fusion(bf16[2048,2560]{1,0:T(8,128)(2,1)} %all-gather.5.cloned.1.call-done, bf16[304,1,2560]{2,1,0:T(2,128)(2,1)} %get-tuple-element.15), kind=kOutput, calls=%fused_computation.16 | convolution fusion | flops 3187671040 | bytes 14532608 | tf_op jit(solution)/shard_map/td,fd->tf/dot_general | solution.py:40
  203.2 15.3 %convolution_convert_fusion = bf16[2048,2560]{1,0:T(8,128)(2,1)} fusion(bf16[304,2560]{1,0:T(8,128)(2,1)S(1)} %reshape.257, bf16[2048,2560]{1,0:T(8,128)(2,1)} %all-gather.5.cloned.1.call-done, f32[2048,304]{0,1:T(8,128)} %fusion.7, bf16[304,1,2560]{2,1,0:T(2,128)(2,1)} %get-tuple-element.14), kind=kOutput, calls=%fused_computation.1 | convolution fusion | flops 6384320512 | bytes 26574848 | tf_op jit(solution)/shard_map/dot_general | solution.py:43
  218.5 1.0 slice.58
  219.7 1.3 scatter_fusion
  221.0 0.9 copy.62
  221.9 94.3 %reduce-scatter.5.cloned.1.call-done = bf16[64,2560]{1,0:T(8,128)(2,1)} async-done(((bf16[2048,2560]{1,0:T(8,128)(2,1)}), bf16[64,2560]{1,0:T(8,128)(2,1)}) %reduce-scatter.5.cloned.1.call-update) | async-done | bytes 327696 | tf_op jit(solution)/shard_map/reduce_scatter | solution.py:105
  316.2 1.8 add_convert_fusion.1
  (49 shorter events, 4.8 us)
Async XLA Ops:
  7.2 56.6 %reduce-scatter.3.cloned.1.call-start = ((), (), s32[]{:S(2)}) async-start(), calls=%async_computation.2 | async-start | bytes 3276800 | tf_op jit(solution)/shard_map/reduce_scatter | solution.py:88
  14.8 1.1 copy-start.2
  14.8 1.4 copy-start.6
  16.2 2.1 copy-start.4
  16.6 2.9 copy-start.5
  21.2 2.3 slice-start
  21.2 2.6 slice-start.1
  26.9 36.9 %copy-start.1 = (bf16[256,2560]{1,0:T(8,128)(2,1)S(1)}, bf16[256,2560]{1,0:T(8,128)(2,1)}, u32[]{:S(2)}) copy-start(bf16[256,2560]{1,0:T(8,128)(2,1)} %param.11) | copy-start | bytes 3932164
  26.9 38.2 %copy-start.3 = (f32[2560]{0:T(1024)S(1)}, f32[2560]{0:T(1024)}, u32[]{:S(2)}) copy-start(f32[2560]{0:T(1024)} %param.19) | copy-start | bytes 30724
  26.9 65.3 %all-gather.9.cloned.1.call-start = ((), (), s32[]{:S(2)}) async-start(), calls=%async_computation.6 | async-start | bytes 2048000 | tf_op jit(solution)/shard_map/all_gather | solution.py:101
  27.6 105.5 %all-gather.7.cloned.1.call-start = ((), (), s32[]{:S(2)}) async-start(), calls=%async_computation.4 | async-start | bytes 3891200 | tf_op jit(solution)/shard_map/all_gather | solution.py:100
  28.4 165.0 %all-gather.5.cloned.1.call-start = ((), (), s32[]{:S(2)}) async-start(), calls=%async_computation.3 | async-start | bytes 10813440 | tf_op jit(solution)/shard_map/all_gather | solution.py:103
  67.0 249.2 %reduce-scatter.5.cloned.1.call-start = ((), (), s32[]{:S(2)}) async-start(), calls=%async_computation.5 | async-start | bytes 10813440 | tf_op jit(solution)/shard_map/reduce_scatter | solution.py:105
  218.5 1.2 copy-start.7
  218.5 97.7 %copy-start = (f32[64,2560]{1,0:T(8,128)S(1)}, f32[64,2560]{1,0:T(8,128)}, u32[]{:S(2)}) copy-start(f32[64,2560]{1,0:T(8,128)} %reduce-scatter.3.cloned.1.call-done) | copy-start | bytes 1966084
Sparse Core Ops, SparseCore 0:
  27.0 36.7 reduce-scatter.2
  65.4 26.7 all-gather.8
  93.9 39.1 all-gather.6
  135.8 57.5 all-gather.4
  218.6 97.5 reduce-scatter.4
where the time goes:
time: 325 us
  waiting for transfers between devices  246 us (76%)
  matrix products  36.6 us (11%)
  local copies, waits for them, and re-layouts  16.8 us (5%)
  between operations  14 us (4%)
  other arithmetic  10.5 us (3%)
    reduce_scatter x1, waiting for transfers between devices, per_device(): lax.psum_scatter(feed_forward(piece, unit_pairs, unit_down).astype(jnp.bf...  94.3 us
    all_gather x1, waiting for transfers between devices, per_device(): gathered = lax.all_gather(mlp_in, 'req', axis=0, tiled=True)  50.8 us
    all_gather x1, waiting for transfers between devices, per_device(): lax.all_gather(gate_up, 'mlp', axis=0, tiled=True)  39.3 us
    reduce_scatter x1, waiting for transfers between devices, per_device(): lax.psum_scatter(jnp.dot(piece, o_weight, preferred_element_type=jnp.floa...  35.3 us
    all_gather x1, waiting for transfers between devices, per_device(): lax.all_gather(down_weight, 'mlp', axis=0, tiled=True)  25 us
    dot_general x1, matrix products, feed_forward(): return jnp.dot(act, unit_down, preferred_element_type=jnp.float32)  15.3 us
    dot_general x1, matrix products, feed_forward(): jnp.einsum('td,fd->tf', rows, unit_pairs[:, 0, :], preferred_element_type...  9.78 us
    slice x1, local copies, waits for them, and re-layouts, feed_forward(): unit_pairs[:, 1, :]  9.43 us
  transfers between devices with their start and end apart: 5, of which 5 were waited for; matrix products, arithmetic and copies ran while one was open for 5% of the time, Pallas kernels for 0%

commit v1 on v0

--- a/solution.py
+++ b/solution.py
@@ -6,6 +6,13 @@
 
 rope_theta = 1000000.0
 norm_eps = 1e-06
+
+
+def exchange_gather(array, axis, dim):
+    size = lax.axis_size(axis)
+    tiles = jnp.stack([array for _ in range(size)])
+    tiles = lax.all_to_all(tiles, axis, split_axis=0, concat_axis=0)
+    return jnp.concatenate(tiles, axis=dim)
 
 
 def rms_scale(values, gain):
@@ -98,7 +105,7 @@
     mlp_in = rms_scale(resid, mlp_norm).astype(jnp.bfloat16)
     unit_pairs, unit_down = (
         lax.all_gather(gate_up, "mlp", axis=0, tiled=True),
-        lax.all_gather(down_weight, "mlp", axis=0, tiled=True),
+        exchange_gather(down_weight, "mlp", 0),
     )
     gathered = lax.all_gather(mlp_in, "req", axis=0, tiled=True)
     piece = gathered

time: 325 us -> 308 us (0.948)
  waiting for transfers between devices: 246 us -> 192 us
  blocking collectives: 0 us -> 37.3 us
    all_to_all x0 -> x1, blocking collectives: none -> 37.3 us  [exchange_gather(): tiles = lax.all_to_all(tiles, axis, split_axis=0, concat_axis=0)]
    all_gather x1, waiting for transfers between devices: 39.3 us -> 10.5 us  [per_device(): lax.all_gather(gate_up, 'mlp', axis=0, tiled=True)]
    all_gather x1 -> x0, waiting for transfers between devices: 25 us -> none  [per_device(): lax.all_gather(down_weight, 'mlp', axis=0, tiled=True)]
  transfers between devices with their start and end apart: 5 -> 4, of which waited for: 5 -> 4; matrix products, arithmetic and copies ran while one was open for 5% -> 6% of each run, Pallas kernels for 0% -> 0%
where the time goes in v1:
time: 308 us
  waiting for transfers between devices  192 us (62%)
  blocking collectives  37.3 us (12%)
  matrix products  36.8 us (12%)
  local copies, waits for them, and re-layouts  16.7 us (5%)
  between operations  14 us (5%)
  other arithmetic  10.5 us (3%)
    reduce_scatter x1, waiting for transfers between devices, per_device(): lax.psum_scatter(feed_forward(piece, unit_pairs, unit_down).astype(jnp.bf...  94.3 us
    all_gather x1, waiting for transfers between devices, per_device(): gathered = lax.all_gather(mlp_in, 'req', axis=0, tiled=True)  50.5 us
    all_to_all x1, blocking collectives, exchange_gather(): tiles = lax.all_to_all(tiles, axis, split_axis=0, concat_axis=0)  37.3 us
    reduce_scatter x1, waiting for transfers between devices, per_device(): lax.psum_scatter(jnp.dot(piece, o_weight, preferred_element_type=jnp.floa...  36 us
    dot_general x1, matrix products, feed_forward(): return jnp.dot(act, unit_down, preferred_element_type=jnp.float32)  15.3 us
    all_gather x1, waiting for transfers between devices, per_device(): lax.all_gather(gate_up, 'mlp', axis=0, tiled=True)  10.5 us
    dot_general x1, matrix products, feed_forward(): jnp.einsum('td,fd->tf', rows, unit_pairs[:, 0, :], preferred_element_type...  9.9 us
    slice x1, local copies, waits for them, and re-layouts, feed_forward(): unit_pairs[:, 1, :]  9.43 us
  transfers between devices with their start and end apart: 4, of which 4 were waited for; matrix products, arithmetic and copies ran while one was open for 6% of the time, Pallas kernels for 0%

profile of v1, /device:TPU:0, one launch (start us, length us, event | category | flops | bytes accessed | tf_op | source)
XLA Modules:
  0.0 307.6 jit_solution(9309065574292001811)
XLA Ops:
  7.2 1.7 fusion.3
  8.9 5.9 %fusion = f32[256,2,768]{2,0,1:T(8,128)S(1)} fusion(bf16[2560,2,768]{2,1,0:T(2,128)(2,1)} %param.15, bf16[256,2560]{1,0:T(8,128)(2,1)} %param.11, f32[2560]{0:T(1024)} %param.14, f32[256]{0:T(256)S(1)} %add_rsqrt_fusion.2), kind=kOutput, calls=%fused_computation.2 | convolution fusion | flops 2015887360 | bytes 10759168 | tf_op jit(solution)/shard_map/sd,dkc->skc/dot_general | solution.py:75
  15.0 1.0 copy-done.2
  17.0 0.6 multiply_reduce_fusion
  18.3 1.1 multiply_multiply_fusion
  20.4 0.9 fusion.6
  21.2 1.7 convolution_convert_fusion.1
  23.8 3.1 fusion.30
  26.9 0.7 all-gather.5.cloned.1.call-update
  27.7 36.0 %reduce-scatter.3.cloned.1.call-done = f32[64,2560]{1,0:T(8,128)} async-done(((f32[256,2560]{1,0:T(8,128)}), f32[64,2560]{1,0:T(8,128)}) %reduce-scatter.3.cloned.1.call-update) | async-done | bytes 655376 | tf_op jit(solution)/shard_map/reduce_scatter | solution.py:95
  63.7 1.3 multiply_reduce_fusion.1
  65.0 1.9 multiply_convert_fusion
  67.2 37.3 %all_to_all.5 = bf16[4,76,2560]{2,1,0:T(8,128)(2,1)S(1)} all-to-all(bf16[4,76,2560]{2,1,0:T(8,128)(2,1)S(1)} %stack.4), channel_id=1, replica_groups=mesh['req'=32,'mlp'=4] {'mlp'}, dimensions={0} | all-to-all | bytes 3112960 | tf_op jit(solution)/shard_map/all_to_all | solution.py:14
  104.5 1.3 reshape.253
  105.8 10.5 %all-gather.5.cloned.1.call-done = bf16[304,2,2560]{2,1,0:T(2,128)(2,1)} async-done(((bf16[76,2,2560]{2,1,0:T(2,128)(2,1)}), bf16[304,2,2560]{2,1,0:T(2,128)(2,1)}) %all-gather.5.cloned.1.call-update) | async-done | bytes 3112976 | tf_op jit(solution)/shard_map/all_gather | solution.py:107
  116.4 9.4 %fusion.27 = (bf16[304,1,2560]{2,1,0:T(2,128)(2,1)}, bf16[304,1,2560]{2,1,0:T(2,128)(2,1)}) fusion(bf16[304,2,2560]{2,1,0:T(2,128)(2,1)} %all-gather.5.cloned.1.call-done), kind=kLoop, calls=%fused_computation.66 | loop fusion | bytes 6225920 | tf_op jit(solution)/shard_map/slice | solution.py:48
  125.8 50.5 %all-gather.3.cloned.1.call-done = bf16[2048,2560]{1,0:T(8,128)(2,1)} async-done(((bf16[64,2560]{1,0:T(8,128)(2,1)}), bf16[2048,2560]{1,0:T(8,128)(2,1)}) %all-gather.3.cloned.1.call-update) | async-done | bytes 10485776 | tf_op jit(solution)/shard_map/all_gather | solution.py:110
  176.3 9.9 %fusion.7 = f32[2048,304]{0,1:T(8,128)} fusion(bf16[2048,2560]{1,0:T(8,128)(2,1)} %all-gather.3.cloned.1.call-done, bf16[304,1,2560]{2,1,0:T(2,128)(2,1)} %get-tuple-element.15), kind=kOutput, calls=%fused_computation.16 | convolution fusion | flops 3187671040 | bytes 14532608 | tf_op jit(solution)/shard_map/td,fd->tf/dot_general | solution.py:47
  186.2 15.3 %convolution_convert_fusion = bf16[2048,2560]{1,0:T(8,128)(2,1)} fusion(bf16[304,2560]{1,0:T(8,128)(2,1)S(1)} %copy-done.3, bf16[2048,2560]{1,0:T(8,128)(2,1)} %all-gather.3.cloned.1.call-done, f32[2048,304]{0,1:T(8,128)} %fusion.7, bf16[304,1,2560]{2,1,0:T(2,128)(2,1)} %get-tuple-element.14), kind=kOutput, calls=%fused_computation.1 | convolution fusion | flops 6384320512 | bytes 26574848 | tf_op jit(solution)/shard_map/dot_general | solution.py:50
  201.6 1.0 slice.58
  202.8 1.3 scatter_fusion
  204.1 0.9 copy.62
  205.0 94.3 %reduce-scatter.5.cloned.1.call-done = bf16[64,2560]{1,0:T(8,128)(2,1)} async-done(((bf16[2048,2560]{1,0:T(8,128)(2,1)}), bf16[64,2560]{1,0:T(8,128)(2,1)}) %reduce-scatter.5.cloned.1.call-update) | async-done | bytes 327696 | tf_op jit(solution)/shard_map/reduce_scatter | solution.py:112
  299.2 1.8 add_convert_fusion.1
  (52 shorter events, 4.1 us)
Async XLA Ops:
  7.2 56.6 %reduce-scatter.3.cloned.1.call-start = ((), (), s32[]{:S(2)}) async-start(), calls=%async_computation.3 | async-start | bytes 3276800 | tf_op jit(solution)/shard_map/reduce_scatter | solution.py:95
  14.8 1.1 copy-start.2
  14.8 1.4 copy-start.8
  16.2 2.1 copy-start.6
  16.6 2.9 copy-start.7
  21.2 2.3 slice-start
  21.2 2.6 slice-start.1
  26.9 36.9 %copy-start.1 = (bf16[256,2560]{1,0:T(8,128)(2,1)S(1)}, bf16[256,2560]{1,0:T(8,128)(2,1)}, u32[]{:S(2)}) copy-start(bf16[256,2560]{1,0:T(8,128)(2,1)} %param.11) | copy-start | bytes 3932164
  26.9 38.2 %copy-start.5 = (f32[2560]{0:T(1024)S(1)}, f32[2560]{0:T(1024)}, u32[]{:S(2)}) copy-start(f32[2560]{0:T(1024)} %param.19) | copy-start | bytes 30724
  26.9 40.2 %copy-start.4 = (bf16[76,2560]{1,0:T(8,128)(2,1)S(1)}, bf16[76,2560]{1,0:T(8,128)(2,1)}, u32[]{:S(2)}) copy-start(bf16[76,2560]{1,0:T(8,128)(2,1)} %param.21) | copy-start | bytes 1167364
  26.9 89.5 %all-gather.5.cloned.1.call-start = ((), (), s32[]{:S(2)}) async-start(), calls=%async_computation.5 | async-start | bytes 3891200 | tf_op jit(solution)/shard_map/all_gather | solution.py:107
  27.6 148.7 %all-gather.3.cloned.1.call-start = ((), (), s32[]{:S(2)}) async-start(), calls=%async_computation.4 | async-start | bytes 10813440 | tf_op jit(solution)/shard_map/all_gather | solution.py:110
  67.0 232.2 %reduce-scatter.5.cloned.1.call-start = ((), (), s32[]{:S(2)}) async-start(), calls=%async_computation.6 | async-start | bytes 10813440 | tf_op jit(solution)/shard_map/reduce_scatter | solution.py:112
  176.3 9.9 %copy-start.3 = (bf16[304,2560]{1,0:T(8,128)(2,1)S(1)}, bf16[304,2560]{1,0:T(8,128)(2,1)}, u32[]{:S(2)}) copy-start(bf16[304,2560]{1,0:T(8,128)(2,1)} %reshape.253) | copy-start | bytes 4669444
  201.5 1.2 copy-start.9
  201.5 97.7 %copy-start = (f32[64,2560]{1,0:T(8,128)S(1)}, f32[64,2560]{1,0:T(8,128)}, u32[]{:S(2)}) copy-start(f32[64,2560]{1,0:T(8,128)} %reduce-scatter.3.cloned.1.call-done) | copy-start | bytes 1966084
Sparse Core Ops, SparseCore 0:
  27.0 36.6 reduce-scatter.2
  65.4 50.9 all-gather.4
  119.2 57.0 all-gather.2
  201.7 97.5 reduce-scatter.4
